TPU v7x, 32 devices: a whole 2x2x4 slice. The times are simulated.
32 devices in a mesh: row: 2 (over x), col: 8 (over z, y), rep: 2 (over core).
Axes of the slice: x: 2, y: 2, z: 4, core: 2. Of those that a mesh axis runs over, the one named last changes fastest.
Arguments:
- vectors: bfloat16 [128, 2048], P('rep', ('row', 'col')), may hold values from -6 to 6
- tile_values: bfloat16 [2304, 128, 128], P(('row', 'col')), may hold values from -6 to 6
- tile_rows: int32 [2304], P(('row', 'col')), may hold values from 0 to 7
- tile_cols: int32 [2304], P(('row', 'col')), may hold values from 0 to 1
- tile_scales: float32 [2304], P(('row', 'col')), may hold values from 0.5 to 2
- live_tiles: int32 [16], P(('row', 'col')), may hold values from 1 to 144, as said below
Outputs:
- basis: float32 [128, 2048], P('rep', ('row', 'col'))
- ritz: float32 [128, 128], replicated
Inputs may be any that keep to these rules, and one draw needn't show every extreme that they name: `live_tiles`: some pair of row and col indices has all 144 of its slots filled.
All inputs are finite; a program needn't handle non-finite values.
Results may differ from a plain program's by a relative error of at most 0.03.
Values may be sent and summed in bfloat16 or wider, within the bound.
A program may use at most 64 MiB of HBM per device.

v0:
```python
import math

import jax
import jax.numpy as jnp
from jax import lax
from jax.sharding import PartitionSpec as P

DEGREE = 3


HIGHEST = lax.Precision.HIGHEST


def slot_weights(rows_here, scales_here, live_here, row_blocks):
    slots = jnp.arange(rows_here.shape[0], dtype=jnp.int32)
    alive = (slots < live_here).astype(jnp.float32)
    onehot = (rows_here[None, :] == jnp.arange(row_blocks, dtype=jnp.int32)[:, None]).astype(
        jnp.float32
    )
    return onehot * (scales_here * alive)[None, :]


def shards(vectors, tile_values, tile_rows, tile_cols, tile_scales, live_tiles):
    half_vec, local_rows = vectors.shape
    block_size = tile_values.shape[1]
    slot_count = tile_values.shape[0]
    local_blocks = local_rows // block_size
    col_size = lax.axis_size("col")
    row_size = lax.axis_size("row")
    row_blocks = col_size * local_blocks
    panel_blocks = row_size * local_blocks
    weights = slot_weights(tile_rows, tile_scales, live_tiles[0], row_blocks)
    absolute = jnp.sum(jnp.abs(tile_values), axis=2, dtype=jnp.float32)
    degree_terms = jnp.dot(weights, absolute, precision=HIGHEST)
    degree_sums = lax.psum_scatter(degree_terms, "col", scatter_dimension=0, tiled=True)
    inv_root = lax.rsqrt(1.0 + degree_sums.reshape(local_rows))

    def apply_operator(current):
        gathered = lax.all_gather(current, "row", axis=1, tiled=True)
        column_set = gathered.reshape(half_vec, panel_blocks, block_size).transpose(1, 0, 2)
        picked = column_set[tile_cols]
        products = jnp.einsum(
            "tkj,tij->tki", picked, tile_values, preferred_element_type=jnp.float32
        )
        flat_products = products.reshape(slot_count, half_vec * block_size)
        summed = lax.psum_scatter(
            jnp.dot(weights, flat_products, precision=HIGHEST)
            .reshape(local_blocks * lax.axis_size("col"), half_vec, block_size)
            .astype(jnp.bfloat16),
            "col",
            scatter_dimension=0,
            tiled=True,
        ).astype(jnp.float32)
        summed = summed.transpose(1, 0, 2).reshape(half_vec, local_rows)
        return summed * inv_root[None, :]

    previous = vectors
    current = apply_operator(previous).astype(jnp.bfloat16)
    for index in range(DEGREE - 1):
        following = (2.0 * apply_operator(current) - previous.astype(jnp.float32)).astype(
            jnp.bfloat16
        )
        previous, current = (current, following)
    image = apply_operator(current)
    rep_index = lax.axis_index("rep")
    all_float, all_image = (
        lax.all_gather(
            current.astype(jnp.float32).astype(jnp.bfloat16), "rep", axis=0, tiled=True
        ).astype(jnp.float32),
        lax.all_gather(image.astype(jnp.bfloat16), "rep", axis=0, tiled=True).astype(image.dtype),
    )
    gram_local = jnp.dot(all_float, all_float.T, precision=HIGHEST)
    cross_local = jnp.dot(all_float, all_image.T, precision=HIGHEST)
    gram, cross = lax.psum((gram_local, cross_local), ("row", "col"))
    lower = jnp.linalg.cholesky(gram)
    factor = math.sqrt(local_rows * row_size * col_size)
    solved = jax.scipy.linalg.solve_triangular(lower, all_float, lower=True)
    basis = factor * lax.dynamic_slice_in_dim(solved, rep_index * half_vec, half_vec, 0)
    left_solved = jax.scipy.linalg.solve_triangular(lower, cross, lower=True)
    ritz = factor * jax.scipy.linalg.solve_triangular(lower, left_solved.T, lower=True).T
    return (basis, ritz)


def solution(mesh):
    return jax.shard_map(
        shards,
        mesh=mesh,
        in_specs=(
            P("rep", ("row", "col")),
            P(("row", "col"), None, None),
            P(("row", "col")),
            P(("row", "col")),
            P(("row", "col")),
            P(("row", "col")),
        ),
        out_specs=(P("rep", ("row", "col")), P()),
        check_vma=False,
    )
```

profile of v0, /device:TPU:0, one launch (start us, length us, event | category | flops | bytes accessed | tf_op | source)
XLA Modules:
  0.0 471.4 jit_solution(8131757096260403358)
XLA Ops:
  8.5 5.6 %all_gather.18 = bf16[64,256]{1,0:T(8,128)(2,1)S(1)} all-gather(bf16[64,128]{1,0:T(8,128)(2,1)} %param.8), channel_id=1, replica_groups=mesh['row'=2,'col'=8,'rep'=2] {'row'}, dimensions={1}, use_global_device_ids=true | all-gather | bytes 49152 | tf_op jit(solution)/shard_map/all_gather | solution.py:39
  14.9 1.0 gather_fusion
  15.9 5.1 %fusion.64 = f32[144,64,128]{2,1,0:T(8,128)S(1)} fusion(bf16[144,64,128]{2,1,0:T(8,128)(2,1)S(1)} %gather_fusion, bf16[144,128,128]{2,1,0:T(8,128)(2,1)} %param.9), kind=kOutput, calls=%fused_computation.88 | convolution fusion | flops 301989888 | bytes 11796480 | tf_op jit(solution)/shard_map/tkj,tij->tki/dot_general | solution.py:42
  21.0 4.9 %fusion.12 = bf16[8,64,128]{2,0,1:T(8,128)(2,1)S(1)} fusion(f32[144]{0:T(256)S(1)} %compare_select_fusion.1, s32[144]{0:T(256)S(1)} %copy-done.2, f32[18,8,64,128]{3,2,1,0:T(8,128)S(1)} %bitcast.150), kind=kOutput, calls=%fused_computation.21 | convolution fusion | flops 113314048 | bytes 4850816 | tf_op jit(solution)/shard_map/dot_general | solution.py:47
  26.6 3.7 convert_reduce_fusion
  31.1 22.2 %all-reduce = f32[8,128]{1,0:T(8,128)S(1)} all-reduce(f32[8,128]{1,0:T(8,128)S(1)} %fusion.40), channel_id=3, replica_groups=mesh['row'=2,'col'=8,'rep'=2] {'col'}, use_global_device_ids=true, to_apply=%region_2.0.clone | all-reduce | flops 1024 | bytes 8192
  53.9 36.8 %reduce-scatter.5.cloned.1.call-done = bf16[1,64,128]{2,1,0:T(8,128)(2,1)} async-done(((bf16[8,64,128]{2,1,0:T(8,128)(2,1)}), bf16[1,64,128]{2,1,0:T(8,128)(2,1)}) %reduce-scatter.5.cloned.1.call-update) | async-done | bytes 16400 | tf_op jit(solution)/shard_map/reduce_scatter | solution.py:46
  91.4 4.6 all_gather.19
  96.0 1.0 gather_fusion.1
  97.0 5.1 %fusion.65 = f32[144,64,128]{2,1,0:T(8,128)S(1)} fusion(bf16[144,64,128]{2,1,0:T(8,128)(2,1)S(1)} %gather_fusion.1, bf16[144,128,128]{2,1,0:T(8,128)(2,1)} %param.9), kind=kOutput, calls=%fused_computation.89 | convolution fusion | flops 301989888 | bytes 11796480 | tf_op jit(solution)/shard_map/tkj,tij->tki/dot_general | solution.py:42
  102.2 4.9 %fusion.15 = bf16[8,64,128]{2,0,1:T(8,128)(2,1)S(1)} fusion(f32[144]{0:T(256)S(1)} %compare_select_fusion.1, s32[144]{0:T(256)S(1)} %copy-done.2, f32[18,8,64,128]{3,2,1,0:T(8,128)S(1)} %bitcast.151), kind=kOutput, calls=%fused_computation.22 | convolution fusion | flops 113314048 | bytes 4850816 | tf_op jit(solution)/shard_map/dot_general | solution.py:47
  107.8 61.3 %reduce-scatter.7.cloned.1.call-done = bf16[1,64,128]{2,1,0:T(8,128)(2,1)} async-done(((bf16[8,64,128]{2,1,0:T(8,128)(2,1)}), bf16[1,64,128]{2,1,0:T(8,128)(2,1)}) %reduce-scatter.7.cloned.1.call-update) | async-done | bytes 16400 | tf_op jit(solution)/shard_map/reduce_scatter | solution.py:46
  169.8 4.7 all_gather.20
  174.5 1.0 gather_fusion.2
  175.5 5.1 %fusion.66 = f32[144,64,128]{2,1,0:T(8,128)S(1)} fusion(bf16[144,64,128]{2,1,0:T(8,128)(2,1)S(1)} %gather_fusion.2, bf16[144,128,128]{2,1,0:T(8,128)(2,1)} %param.9), kind=kOutput, calls=%fused_computation.90 | convolution fusion | flops 301989888 | bytes 11796480 | tf_op jit(solution)/shard_map/tkj,tij->tki/dot_general | solution.py:42
  180.6 4.9 %fusion.18 = bf16[8,64,128]{2,0,1:T(8,128)(2,1)S(1)} fusion(f32[144]{0:T(256)S(1)} %compare_select_fusion.1, s32[144]{0:T(256)S(1)} %copy-done.2, f32[18,8,64,128]{3,2,1,0:T(8,128)S(1)} %bitcast.152), kind=kOutput, calls=%fused_computation.23 | convolution fusion | flops 113314048 | bytes 4850816 | tf_op jit(solution)/shard_map/dot_general | solution.py:47
  186.3 61.4 %reduce-scatter.9.cloned.1.call-done = bf16[1,64,128]{2,1,0:T(8,128)(2,1)} async-done(((bf16[8,64,128]{2,1,0:T(8,128)(2,1)}), bf16[1,64,128]{2,1,0:T(8,128)(2,1)}) %reduce-scatter.9.cloned.1.call-update) | async-done | bytes 16400 | tf_op jit(solution)/shard_map/reduce_scatter | solution.py:46
  248.4 4.7 all_gather.22
  253.1 1.0 gather_fusion.3
  254.1 5.1 %fusion.68 = f32[144,64,128]{2,1,0:T(8,128)S(1)} fusion(bf16[144,64,128]{2,1,0:T(8,128)(2,1)S(1)} %gather_fusion.3, bf16[144,128,128]{2,1,0:T(8,128)(2,1)} %param.9), kind=kOutput, calls=%fused_computation.92 | convolution fusion | flops 301989888 | bytes 11796480 | tf_op jit(solution)/shard_map/tkj,tij->tki/dot_general | solution.py:42
  259.2 4.9 %fusion.21 = bf16[8,64,128]{2,0,1:T(8,128)(2,1)S(1)} fusion(f32[144]{0:T(256)S(1)} %compare_select_fusion.1, s32[144]{0:T(256)S(1)} %copy-done.2, f32[18,8,64,128]{3,2,1,0:T(8,128)S(1)} %bitcast.149), kind=kOutput, calls=%fused_computation.24 | convolution fusion | flops 113314048 | bytes 4850816 | tf_op jit(solution)/shard_map/dot_general | solution.py:47
  264.8 1.8 all_gather.21
  266.6 0.8 fusion.67
  267.4 58.8 %reduce-scatter.11.cloned.1.call-done = bf16[1,64,128]{2,1,0:T(8,128)(2,1)} async-done(((bf16[8,64,128]{2,1,0:T(8,128)(2,1)}), bf16[1,64,128]{2,1,0:T(8,128)(2,1)}) %reduce-scatter.11.cloned.1.call-update) | async-done | bytes 16400 | tf_op jit(solution)/shard_map/reduce_scatter | solution.py:46
  326.9 2.1 all_gather.23
  329.0 0.8 fusion.69
  329.8 107.3 %all-reduce.4.cloned.1.call-done = (f32[128,128]{0,1:T(8,128)}, f32[128,128]{1,0:T(8,128)}) async-done(((f32[128,128]{0,1:T(8,128)}, f32[128,128]{1,0:T(8,128)}), (f32[128,128]{0,1:T(8,128)}, f32[128,128]{1,0:T(8,128)})) %all-reduce.4.cloned.1.call-update) | async-done | bytes 131088 | tf_op jit(solution)/shard_map/psum | solution.py:74
  437.1 0.9 copy.105
  438.1 0.9 fusion.30
  438.9 11.7 %cholesky.18 = f32[128,128]{1,0:T(8,128)S(1)} custom-call(f32[128,128]{1,0:T(8,128)S(1)} %fusion.30), custom_call_target="Cholesky" | custom-call | tf_op jit(solution)/shard_map/jit(cholesky)/cholesky | solution.py:75
  452.0 9.8 %custom-call.8 = f32[1,128,128]{1,2,0:T(8,128)S(1)} custom-call(f32[1,128,128]{2,1,0:T(8,128)S(1)} %fusion.25), custom_call_target="InvertDiagBlocksLowerTriangular" | custom-call | tf_op jit(solution)/shard_map/jit(_solve_triangular)/triangular_solve | solution.py:77
  462.1 1.1 convolution_bitcast_fusion
  (43 shorter events, 11.9 us)
Async XLA Ops:
  7.2 83.5 %reduce-scatter.5.cloned.1.call-start = ((), (), s32[]{:S(2)}) async-start(), calls=%async_computation.4 | async-start | bytes 147456 | tf_op jit(solution)/shard_map/reduce_scatter | solution.py:46
  15.9 5.1 %copy-start.2 = (s32[144]{0:T(256)S(1)}, s32[144]{0:T(256)}, u32[]{:S(2)}) copy-start(s32[144]{0:T(256)} %param.10) | copy-start | bytes 1732
  21.0 9.3 %copy-start.3 = (u32[32]{0:T(128)S(1)}, u32[32]{0:T(128)}, u32[]{:S(2)}) copy-start(u32[32]{0:T(128)} %constant.68) | copy-start | bytes 388
  26.6 142.5 %reduce-scatter.7.cloned.1.call-start = ((), (), s32[]{:S(2)}) async-start(), calls=%async_computation.5 | async-start | bytes 147456 | tf_op jit(solution)/shard_map/reduce_scatter | solution.py:46
  102.2 67.0 %copy-start = (bf16[64,128]{1,0:T(8,128)(2,1)S(1)}, bf16[64,128]{1,0:T(8,128)(2,1)}, u32[]{:S(2)}) copy-start(bf16[64,128]{1,0:T(8,128)(2,1)} %param.8) | copy-start | bytes 49156
  107.7 139.9 %reduce-scatter.9.cloned.1.call-start = ((), (), s32[]{:S(2)}) async-start(), calls=%async_computation.6 | async-start | bytes 147456 | tf_op jit(solution)/shard_map/reduce_scatter | solution.py:46
  180.6 67.0 %copy-start.1 = (bf16[1,64,128]{2,1,0:T(8,128)(2,1)S(1)}, bf16[1,64,128]{2,1,0:T(8,128)(2,1)}, u32[]{:S(2)}) copy-start(bf16[1,64,128]{2,1,0:T(8,128)(2,1)} %reduce-scatter.5.cloned.1.call-done) | copy-start | bytes 49156
  186.2 140.0 %reduce-scatter.11.cloned.1.call-start = ((), (), s32[]{:S(2)}) async-start(), calls=%async_computation.7 | async-start | bytes 147456 | tf_op jit(solution)/shard_map/reduce_scatter | solution.py:46
  264.8 172.4 %all-reduce.4.cloned.1.call-start = ((), (), s32[]{:S(2)}) async-start(), calls=%async_computation.8 | async-start | bytes 262144 | tf_op jit(solution)/shard_map/psum | solution.py:74
Sparse Core Ops, SparseCore 0:
  26.7 63.9 reduce-scatter.4
  107.8 61.2 reduce-scatter.6
  186.3 61.2 reduce-scatter.8
  264.9 61.2 reduce-scatter.10
  332.1 104.9 all-reduce.3
where the time goes:
time: 472 us; the launch traced here: 471 us
  waiting for transfers between devices  326 us (69%)
  blocking collectives  45.7 us (10%)
  matrix products  43.3 us (9%)
  other arithmetic  32.9 us (7%)
  between operations  14.6 us (3%)
  local copies, waits for them, and re-layouts  8.97 us (2%)
    reduce_scatter x4, waiting for transfers between devices, apply_operator(): lax.psum_scatter(jnp.dot(weights, flat_products, precision=HIGHEST).resha...  218 us
    psum x1, waiting for transfers between devices, shards(): gram, cross = lax.psum((gram_local, cross_local), ('row', 'col'))  107 us
    unnamed x1, blocking collectives  22.2 us
    dot_general x4, matrix products, apply_operator(): jnp.einsum('tkj,tij->tki', picked, tile_values, preferred_element_type=jn...  20.4 us
    all_gather x4, blocking collectives, apply_operator(): gathered = lax.all_gather(current, 'row', axis=1, tiled=True)  19.6 us
    dot_general x4, matrix products, apply_operator(): jnp.dot(weights, flat_products, precision=HIGHEST)  19.5 us
    another operation x3, other arithmetic, shards(): lower = jnp.linalg.cholesky(gram)  12.4 us
    another operation x2, other arithmetic, shards(): solved = jax.scipy.linalg.solve_triangular(lower, all_float, lower=True)  10.5 us
  transfers between devices with their start and end apart: 5, of which 5 were waited for; matrix products, arithmetic and copies ran while one was open for 1% of the time, Pallas kernels for 0%

commit v1 on v0

v1 whole, which is shorter than its diff:
```python
import functools
import math

import jax
import jax.numpy as jnp
from jax import lax
from jax.experimental import pallas as pl
from jax.experimental.pallas import tpu as pltpu
from jax.sharding import PartitionSpec as P

DEGREE = 3
HIGHEST = lax.Precision.HIGHEST
MESH = pl.DeviceIdType.MESH
F32 = jnp.float32
BF16 = jnp.bfloat16


def pieces_of(count, want):
    while count % want:
        want -= 1
    return want


def assemble(
    row_blocks, panel_blocks, chunks,
    rows_ref, cols_ref, scales_ref, live_ref, rep_ref, tiles_ref,
    high_ref, low_ref, degree_ref, held, total, absolute, sems,
):
    slots, half, block = held.shape
    step = slots // chunks
    copies = []
    first = pl.multiple_of(rep_ref[0] * half, half)
    for c in range(chunks):
        part = pl.ds(c * step, step)
        copy = pltpu.make_async_copy(
            tiles_ref.at[part, pl.ds(first, half), :], held.at[part], sems.at[c]
        )
        copy.start()
        copies.append(copy)
    total[...] = jnp.zeros_like(total)
    absolute[...] = jnp.zeros_like(absolute)
    live = live_ref[0]
    for c in range(chunks):
        copies[c].wait()

        def body(t, carry):
            scale = jnp.where(t < live, scales_ref[t], 0.0)
            row = rows_ref[t]
            values = held[t].astype(F32)
            place = row * panel_blocks + cols_ref[t]
            total[place] = total[place] + values * scale
            absolute[row] = absolute[row] + jnp.abs(values) * scale
            return carry

        lax.fori_loop(c * step, (c + 1) * step, body, 0, unroll=4)
    for r in range(row_blocks):
        for c in range(panel_blocks):
            whole = total[r * panel_blocks + c]
            high = whole.astype(BF16)
            high_ref[r * half : (r + 1) * half, c * block : (c + 1) * block] = high
            low_ref[r * half : (r + 1) * half, c * block : (c + 1) * block] = (
                whole - high.astype(F32)
            ).astype(BF16)
    degree_ref[...] = jnp.zeros_like(degree_ref)
    for p in range(row_blocks // 2):
        pair = absolute[2 * p : 2 * p + 2].reshape(2 * half, block)
        degree_ref[p : p + 1, :] = jnp.sum(pair.T, axis=0, keepdims=True)


def contract(a, b, dims):
    return lax.dot_general(a, b, (dims, ((), ())), preferred_element_type=F32)


def split(value):
    high = value.astype(BF16)
    return high, (value - high.astype(F32)).astype(BF16)


def exchange(
    n_row, n_col, n_rep,
    high_ref, low_ref, degree_ref, vectors_ref,
    gram_ref, cross_ref, block_ref,
    raw, degrees, panels, sends, lands, owners, inv, grams, cross_send, cross_one, cross_two, cross_all,
    g_send, g_recv, c_send, c_recv,
):
    row, col, rep = lax.axis_index("row"), lax.axis_index("col"), lax.axis_index("rep")
    n_group = n_row * n_rep
    me = row * n_rep + rep
    half = vectors_ref.shape[0]
    count = half * n_rep

    def group_peer(k):
        other = lax.rem(me + k, n_group)
        return (lax.div(other, n_rep), col, lax.rem(other, n_rep))

    def col_peer(k):
        return (row, lax.rem(col + k, n_col), rep)

    barrier = pltpu.get_barrier_semaphore()
    for k in range(1, n_group):
        pl.semaphore_signal(barrier, inc=1, device_id=group_peer(k), device_id_type=MESH)
    for k in range(1, n_col):
        pl.semaphore_signal(barrier, inc=1, device_id=col_peer(k), device_id_type=MESH)
    pl.semaphore_wait(barrier, n_group + n_col - 2)

    started = []

    def to_group(phase, source, target):
        out = []
        for k in range(1, n_group):
            copy = pltpu.make_async_remote_copy(
                src_ref=source(lax.rem(me + k, n_group)), dst_ref=target,
                send_sem=g_send.at[phase, k - 1], recv_sem=g_recv.at[phase, k - 1],
                device_id=group_peer(k), device_id_type=MESH,
            )
            copy.start()
            out.append(copy)
        started.extend(out)
        return out

    def to_col(phase, source, target):
        out = []
        order = sorted(range(1, n_col), key=lambda k: -min(k, n_col - k))
        for k in order:
            copy = pltpu.make_async_remote_copy(
                src_ref=source(lax.rem(col + k, n_col)), dst_ref=target,
                send_sem=c_send.at[phase, k - 1], recv_sem=c_recv.at[phase, k - 1],
                device_id=col_peer(k), device_id_type=MESH,
            )
            copy.start()
            out.append(copy)
        started.extend(out)
        return out

    def arrive(copies):
        for copy in copies:
            copy.wait_recv()

    gathering = to_group(0, lambda m: vectors_ref, raw.at[me])
    degree_moves = to_col(0, lambda m: degree_ref, degrees.at[col])
    raw[me] = vectors_ref[...]
    degrees[col] = degree_ref[...]
    arrive(gathering)
    for c in range(n_row):
        whole = jnp.concatenate([raw[c * n_rep + q] for q in range(n_rep)], axis=0)
        turned = whole.astype(F32).T.astype(BF16)
        for q in range(n_rep):
            panels[0, c * n_rep + q] = turned[q * half : (q + 1) * half]

    def products(index):
        panel = panels[index].reshape(n_group * half, count)
        return contract(high_ref[...], panel, ((1,), (0,))) + contract(
            low_ref[...], panel, ((1,), (0,))
        )

    previous = panels[0, me].astype(F32)
    current = previous
    for n in range(DEGREE):
        sends[n] = products(n).astype(BF16).reshape(n_col, half, count)
        moving = to_col(1 + n, lambda m: sends.at[n, m], lands.at[n, col])
        if n == 0:
            arrive(degree_moves)
            sums = degrees[0]
            for s in range(1, n_col):
                sums = sums + degrees[s]
            roots = lax.rsqrt(1.0 + sums)
            padded = jnp.concatenate(
                [roots, jnp.zeros((count - roots.shape[0], roots.shape[1]), F32)], axis=0
            ).T
            for p in range(n_col // 2):
                wide = jnp.broadcast_to(padded[:, p : p + 1], (2 * half, count))
                inv[2 * p] = wide[:half]
                inv[2 * p + 1] = wide[half:]
        lands[n, col] = sends[n, col]
        arrive(moving)
        value = lands[n, 0].astype(F32)
        for s in range(1, n_col):
            value = value + lands[n, s].astype(F32)
        value = value * inv[col]
        if n > 0:
            value = 2.0 * value - previous
        rounded = value.astype(BF16)
        previous, current = current, rounded.astype(F32)
        panels[n + 1, me] = rounded
        if n == DEGREE - 1:
            owners[col] = rounded
            sharing = to_col(DEGREE + 1, lambda m: owners.at[col], owners.at[col])
        gathering = to_group(1 + n, lambda m: panels.at[n + 1, me], panels.at[n + 1, me])
        arrive(gathering)

    images = products(DEGREE) * inv[...].reshape(n_col * half, count)
    block_ref[...] = panels[DEGREE, pl.ds(row * n_rep, n_rep)].reshape(count, count)
    arrive(sharing)
    filtered = owners[...].reshape(n_col * half, count)
    grams[me] = contract(filtered, filtered, ((0,), (0,)))
    gram_moves = to_group(DEGREE + 1, lambda m: grams.at[me], grams.at[me])
    image_high, image_low = split(images)
    cross = contract(filtered, image_high, ((0,), (0,))) + contract(
        filtered, image_low, ((0,), (0,))
    )
    piece = count // n_group
    cross_send[...] = cross.reshape(n_group, piece, count)
    moving = to_group(DEGREE + 2, lambda m: cross_send.at[m], cross_one.at[me])
    cross_one[me] = cross_send[me]
    arrive(moving)
    value = cross_one[0]
    for s in range(1, n_group):
        value = value + cross_one[s]
    cross_two[col] = value
    moving = to_col(DEGREE + 2, lambda m: cross_two.at[col], cross_two.at[col])
    arrive(gram_moves)
    gram = grams[0]
    for s in range(1, n_group):
        gram = gram + grams[s]
    gram_ref[...] = gram
    arrive(moving)
    value = cross_two[0]
    for s in range(1, n_col):
        value = value + cross_two[s]
    cross_all[me] = value
    moving = to_group(DEGREE + 3, lambda m: cross_all.at[me], cross_all.at[me])
    arrive(moving)
    cross_ref[...] = cross_all[...].reshape(count, count)
    for copy in started:
        copy.wait_send()


def finish(n_rep, factor, rep_ref, gram_ref, cross_ref, block_ref, basis_ref, ritz_ref, work, back):
    size = gram_ref.shape[0]
    lines = lax.broadcasted_iota(jnp.int32, (size, size), 0)
    lanes = lax.broadcasted_iota(jnp.int32, (size, size), 1)
    work[...] = gram_ref[...]
    back[...] = (lines == lanes).astype(F32)

    def body(j, carry):
        line = work[pl.ds(j, 1), :]
        other = back[pl.ds(j, 1), :]
        matrix = work[...]
        pivot = jnp.sum(jnp.where(lanes[:1] == j, line, 0.0), axis=1, keepdims=True)
        column = jnp.sum(jnp.where(lanes == j, matrix, 0.0), axis=1, keepdims=True)
        scale = jnp.where(lines[:, :1] > j, column / pivot, 0.0)
        work[...] = matrix - scale * line
        back[...] = back[...] - scale * other
        return carry

    lax.fori_loop(0, size, body, 0)
    diagonal = jnp.sum(jnp.where(lines == lanes, work[...], 0.0), axis=1, keepdims=True)
    back[...] = back[...] * lax.rsqrt(diagonal)
    inverse = back[...]

    def dot(a, b, dims):
        return lax.dot_general(a, b, (dims, ((), ())), precision=HIGHEST, preferred_element_type=F32)

    half = size // n_rep
    own = back[pl.ds(pl.multiple_of(rep_ref[0] * half, half), half), :]
    basis_ref[...] = factor * dot(own, block_ref[...].astype(F32), ((1,), (1,)))
    ritz_ref[...] = factor * dot(dot(inverse, cross_ref[...], ((1,), (0,))), inverse, ((1,), (1,)))


def solution(mesh):
    n_row, n_col, n_rep = (mesh.shape[a] for a in ("row", "col", "rep"))
    n_group = n_row * n_rep
    vmem = pl.BlockSpec(memory_space=pltpu.VMEM)
    smem = pl.BlockSpec(memory_space=pltpu.SMEM)
    shape = jax.ShapeDtypeStruct

    def shards(vectors, tile_values, tile_rows, tile_cols, tile_scales, live_tiles):
        half_vec, local_rows = vectors.shape
        slots, block = tile_values.shape[:2]
        assert local_rows == block and half_vec * n_rep == block
        half = block // n_rep
        count = half_vec * n_rep
        rep = lax.axis_index("rep").astype(jnp.int32).reshape(1)
        chunks = pieces_of(slots, 6)
        lines = -(-(n_col * half // block) // 8) * 8
        high, low, degree = pl.pallas_call(
            functools.partial(assemble, n_col, n_row, chunks),
            out_shape=(
                shape((n_col * half, n_row * block), BF16),
                shape((n_col * half, n_row * block), BF16),
                shape((lines, block), F32),
            ),
            in_specs=[smem] * 5 + [pl.BlockSpec(memory_space=pl.ANY)],
            out_specs=(vmem, vmem, vmem),
            scratch_shapes=[
                pltpu.VMEM((slots, half, block), BF16),
                pltpu.VMEM((n_col * n_row, half, block), F32),
                pltpu.VMEM((n_col, half, block), F32),
                pltpu.SemaphoreType.DMA((chunks,)),
            ],
            name="assemble",
        )(tile_rows, tile_cols, tile_scales, live_tiles, rep, tile_values)
        piece = count // n_group
        gram, cross, filtered = pl.pallas_call(
            functools.partial(exchange, n_row, n_col, n_rep),
            out_shape=(
                shape((count, count), F32), shape((count, count), F32), shape((block, count), BF16),
            ),
            in_specs=[vmem] * 4,
            out_specs=(vmem,) * 3,
            scratch_shapes=[
                pltpu.VMEM((n_group, half_vec, block), BF16),
                pltpu.VMEM((n_col, lines, block), F32),
                pltpu.VMEM((DEGREE + 1, n_group, half, count), BF16),
                pltpu.VMEM((DEGREE, n_col, half, count), BF16),
                pltpu.VMEM((DEGREE, n_col, half, count), BF16),
                pltpu.VMEM((n_col, half, count), BF16),
                pltpu.VMEM((n_col, half, count), F32),
                pltpu.VMEM((n_group, count, count), F32),
                pltpu.VMEM((n_group, piece, count), F32),
                pltpu.VMEM((n_group, piece, count), F32),
                pltpu.VMEM((n_col, piece, count), F32),
                pltpu.VMEM((n_group, piece, count), F32),
                pltpu.SemaphoreType.DMA((DEGREE + 4, n_group - 1)),
                pltpu.SemaphoreType.DMA((DEGREE + 4, n_group - 1)),
                pltpu.SemaphoreType.DMA((DEGREE + 3, n_col - 1)),
                pltpu.SemaphoreType.DMA((DEGREE + 3, n_col - 1)),
            ],
            compiler_params=pltpu.CompilerParams(collective_id=0, has_side_effects=True),
            name="exchange",
        )(high, low, degree, vectors)
        factor = math.sqrt(local_rows * n_row * n_col)
        return pl.pallas_call(
            functools.partial(finish, n_rep, factor),
            out_shape=(shape((half_vec, local_rows), F32), shape((count, count), F32)),
            in_specs=[smem] + [vmem] * 3,
            out_specs=(vmem,) * 2,
            scratch_shapes=[pltpu.VMEM((count, count), F32), pltpu.VMEM((count, count), F32)],
            name="finish",
        )(rep, gram, cross, filtered)

    return jax.shard_map(
        shards,
        mesh=mesh,
        in_specs=(
            P("rep", ("row", "col")),
            P(("row", "col"), None, None),
            P(("row", "col")),
            P(("row", "col")),
            P(("row", "col")),
            P(("row", "col")),
        ),
        out_specs=(P("rep", ("row", "col")), P()),
        check_vma=False,
    )
```

time: 472 us -> 73.1 us (0.15)
  waiting for transfers between devices: 326 us -> 0 us
  Pallas kernels: 0 us -> 71.6 us
  blocking collectives: 45.7 us -> 0 us
  matrix products: 43.3 us -> 0 us
  other arithmetic: 32.9 us -> 0 us
  between operations: 14.6 us -> 1.3 us
  local copies, waits for them, and re-layouts: 8.97 us -> 0 us
    reduce_scatter x4 -> x0, waiting for transfers between devices: 218 us -> none  [apply_operator(): lax.psum_scatter(jnp.dot(weights, flat_products, precision=HIGHEST).resha...]
    psum x1 -> x0, waiting for transfers between devices: 107 us -> none  [shards(): gram, cross = lax.psum((gram_local, cross_local), ('row', 'col'))]
    pallas_call x0 -> x3, Pallas kernels: none -> 71.6 us  [the longest x1 52.2 us: shards(): pl.pallas_call(functools.partial(exchange, n_row, n_col, n_rep), out_shap...]
    dot_general x11 -> x0, matrix products: 41.6 us -> none  [the longest x4 20.4 us: apply_operator(): jnp.einsum('tkj,tij->tki', picked, tile_values, preferred_element_type=jn...]
    all_gather x6 -> x0, blocking collectives: 23.5 us -> none  [the longest x4 19.6 us: apply_operator(): gathered = lax.all_gather(current, 'row', axis=1, tiled=True)]
    another operation x5 -> x0, other arithmetic: 22.9 us -> none  [the longest x3 12.4 us: shards(): lower = jnp.linalg.cholesky(gram)]
    unnamed x1 -> x0, blocking collectives: 22.2 us -> none
  transfers between devices with their start and end apart: 5 -> 0, of which waited for: 5 -> 0; matrix products, arithmetic and copies ran while one was open for 1% -> 0% of each run, Pallas kernels for 0% -> 0%
where the time goes in v1:
time: 73.1 us; the launch traced here: 72.9 us
  Pallas kernels  71.6 us (98%)
  between operations  1.3 us (2%)
    pallas_call x1, Pallas kernels, shards(): pl.pallas_call(functools.partial(exchange, n_row, n_col, n_rep), out_shap...  52.2 us
    pallas_call x1, Pallas kernels, shards(): pl.pallas_call(functools.partial(finish, n_rep, factor), out_shape=(shape...  15.5 us
    pallas_call x1, Pallas kernels, shards(): pl.pallas_call(functools.partial(assemble, n_col, n_row, chunks), out_sha...  3.89 us

profile of v1, /device:TPU:0, one launch (start us, length us, event | category | flops | bytes accessed | tf_op | source)
XLA Modules:
  0.0 72.9 jit_solution(11653890263381206902)
XLA Ops:
  1.3 3.9 %assemble.1 = (bf16[512,256]{1,0:T(8,128)(2,1)}, bf16[512,256]{1,0:T(8,128)(2,1)}, f32[8,128]{1,0:T(8,128)}) custom-call(s32[144]{0:T(256)} %rows_ref.1, s32[144]{0:T(256)} %cols_ref.1, f32[144]{0:T(256)} %scales_ref.1, s32[1]{0:T(128)S(6)} %copy.8.live_ref, s32[1]{0:T(128)} %bitcast.rep_ref, bf16[144,128,128]{2,1,0:T(8,128)(2,1)} %tiles_ref.1), custom_call_target="tpu_custom_call" | custom-call | tf_op jit(solution)/shard_map/assemble/pallas_call | solution.py:276
  5.2 52.2 %exchange.1 = (f32[128,128]{1,0:T(8,128)}, f32[128,128]{1,0:T(8,128)}, bf16[128,128]{1,0:T(8,128)(2,1)}) custom-call(bf16[512,256]{1,0:T(8,128)(2,1)} %get-tuple-element.8.high_ref, bf16[512,256]{1,0:T(8,128)(2,1)} %get-tuple-element.9.low_ref, f32[8,128]{1,0:T(8,128)} %get-tuple-element.10.degree_ref, bf16[64,128]{1,0:T(8,128)(2,1)} %vectors_ref.1), custom_call_target="tpu_custom_call" | custom-call | tf_op jit(solution)/shard_map/exchange/pallas_call | solution.py:294
  57.3 15.5 %finish.1 = (f32[64,128]{1,0:T(8,128)}, f32[128,128]{1,0:T(8,128)}) custom-call(s32[1]{0:T(128)} %bitcast.rep_ref, f32[128,128]{1,0:T(8,128)} %get-tuple-element.11.gram_ref, f32[128,128]{1,0:T(8,128)} %get-tuple-element.12.cross_ref, bf16[128,128]{1,0:T(8,128)(2,1)} %get-tuple-element.13.block_ref), custom_call_target="tpu_custom_call" | custom-call | tf_op jit(solution)/shard_map/finish/pallas_call | solution.py:323

commit v2 on v1

--- a/solution.py
+++ b/solution.py
@@ -9,6 +9,7 @@
 from jax.sharding import PartitionSpec as P
 
 DEGREE = 3
+BAND = 16
 HIGHEST = lax.Precision.HIGHEST
 MESH = pl.DeviceIdType.MESH
 F32 = jnp.float32
@@ -76,11 +77,42 @@
     return high, (value - high.astype(F32)).astype(BF16)
 
 
+def exact(a, b, dims):
+    return lax.dot_general(a, b, (dims, ((), ())), precision=HIGHEST, preferred_element_type=F32)
+
+
+def eliminate(work, inverse, band):
+    size = work.shape[0]
+    base = band * BAND
+    left = work[base : base + BAND, :size]
+    right = work[base : base + BAND, size:]
+    places = lax.broadcasted_iota(jnp.int32, (BAND, size), 0)
+    columns = [
+        jnp.broadcast_to(left[:, base + j : base + j + 1], (BAND, size)) for j in range(BAND)
+    ]
+    for j in range(BAND):
+        root = lax.rsqrt(columns[j][j : j + 1])
+        scaled = columns[j] * root
+        for k in range(j + 1, BAND):
+            columns[k] = columns[k] - scaled * scaled[k : k + 1]
+        below = jnp.where(places > j, scaled, 0.0)
+        factor = jnp.where(places == j, root, 1.0)
+        left = left * factor
+        right = right * factor
+        left = left - below * left[j : j + 1]
+        right = right - below * right[j : j + 1]
+    inverse[base : base + BAND, :] = right
+    if base + BAND < size:
+        rows = jnp.concatenate([left, right], axis=1)
+        change = exact(left, rows, ((0,), (0,)))
+        work[base + BAND :, :] = work[base + BAND :, :] - change[base + BAND :, :]
+
+
 def exchange(
-    n_row, n_col, n_rep,
+    n_row, n_col, n_rep, factor,
     high_ref, low_ref, degree_ref, vectors_ref,
-    gram_ref, cross_ref, block_ref,
-    raw, degrees, panels, sends, lands, owners, inv, grams, cross_send, cross_one, cross_two, cross_all,
+    basis_ref, ritz_ref,
+    raw, degrees, panels, sends, lands, owners, inv, grams, cross_send, cross_one, cross_two, cross_all, work, inverse,
     g_send, g_recv, c_send, c_recv,
 ):
     row, col, rep = lax.axis_index("row"), lax.axis_index("col"), lax.axis_index("rep")
@@ -120,12 +152,14 @@
 
     def to_col(phase, source, target):
         out = []
-        order = sorted(range(1, n_col), key=lambda k: -min(k, n_col - k))
-        for k in order:
+        upper = lax.div(2 * col, n_col)
+        for s in range(n_col - 1):
+            k = (1 - upper) * (n_col - 1 - s) + upper * (1 + s)
+            other = lax.rem(col + k, n_col)
             copy = pltpu.make_async_remote_copy(
-                src_ref=source(lax.rem(col + k, n_col)), dst_ref=target,
+                src_ref=source(other), dst_ref=target,
                 send_sem=c_send.at[phase, k - 1], recv_sem=c_recv.at[phase, k - 1],
-                device_id=col_peer(k), device_id_type=MESH,
+                device_id=(row, other, rep), device_id_type=MESH,
             )
             copy.start()
             out.append(copy)
@@ -189,7 +223,6 @@
         arrive(gathering)
 
     images = products(DEGREE) * inv[...].reshape(n_col * half, count)
-    block_ref[...] = panels[DEGREE, pl.ds(row * n_rep, n_rep)].reshape(count, count)
     arrive(sharing)
     filtered = owners[...].reshape(n_col * half, count)
     grams[me] = contract(filtered, filtered, ((0,), (0,)))
@@ -200,61 +233,44 @@
     )
     piece = count // n_group
     cross_send[...] = cross.reshape(n_group, piece, count)
-    moving = to_group(DEGREE + 2, lambda m: cross_send.at[m], cross_one.at[me])
+    cross_moves = to_group(DEGREE + 2, lambda m: cross_send.at[m], cross_one.at[me])
     cross_one[me] = cross_send[me]
-    arrive(moving)
+    arrive(gram_moves)
+    gram = grams[0]
+    for s in range(1, n_group):
+        gram = gram + grams[s]
+    work[:, :count] = gram
+    work[:, count:] = (
+        lax.broadcasted_iota(jnp.int32, (count, count), 0)
+        == lax.broadcasted_iota(jnp.int32, (count, count), 1)
+    ).astype(F32)
+    bands = count // BAND
+    eliminate(work, inverse, 0)
+    arrive(cross_moves)
     value = cross_one[0]
     for s in range(1, n_group):
         value = value + cross_one[s]
     cross_two[col] = value
     moving = to_col(DEGREE + 2, lambda m: cross_two.at[col], cross_two.at[col])
-    arrive(gram_moves)
-    gram = grams[0]
-    for s in range(1, n_group):
-        gram = gram + grams[s]
-    gram_ref[...] = gram
+    for band in range(1, bands - 2):
+        eliminate(work, inverse, band)
     arrive(moving)
     value = cross_two[0]
     for s in range(1, n_col):
         value = value + cross_two[s]
     cross_all[me] = value
     moving = to_group(DEGREE + 3, lambda m: cross_all.at[me], cross_all.at[me])
+    for band in range(bands - 2, bands):
+        eliminate(work, inverse, band)
+    block = panels[DEGREE, pl.ds(row * n_rep, n_rep)].reshape(count, count).astype(F32)
+    own = inverse[pl.ds(pl.multiple_of(rep * half, half), half), :]
+    basis_ref[...] = factor * exact(own, block, ((1,), (1,)))
+    whole = inverse[...]
     arrive(moving)
-    cross_ref[...] = cross_all[...].reshape(count, count)
+    left = exact(whole, cross_all[...].reshape(count, count), ((1,), (0,)))
+    ritz_ref[...] = factor * exact(left, whole, ((1,), (1,)))
     for copy in started:
         copy.wait_send()
-
-
-def finish(n_rep, factor, rep_ref, gram_ref, cross_ref, block_ref, basis_ref, ritz_ref, work, back):
-    size = gram_ref.shape[0]
-    lines = lax.broadcasted_iota(jnp.int32, (size, size), 0)
-    lanes = lax.broadcasted_iota(jnp.int32, (size, size), 1)
-    work[...] = gram_ref[...]
-    back[...] = (lines == lanes).astype(F32)
-
-    def body(j, carry):
-        line = work[pl.ds(j, 1), :]
-        other = back[pl.ds(j, 1), :]
-        matrix = work[...]
-        pivot = jnp.sum(jnp.where(lanes[:1] == j, line, 0.0), axis=1, keepdims=True)
-        column = jnp.sum(jnp.where(lanes == j, matrix, 0.0), axis=1, keepdims=True)
-        scale = jnp.where(lines[:, :1] > j, column / pivot, 0.0)
-        work[...] = matrix - scale * line
-        back[...] = back[...] - scale * other
-        return carry
-
-    lax.fori_loop(0, size, body, 0)
-    diagonal = jnp.sum(jnp.where(lines == lanes, work[...], 0.0), axis=1, keepdims=True)
-    back[...] = back[...] * lax.rsqrt(diagonal)
-    inverse = back[...]
-
-    def dot(a, b, dims):
-        return lax.dot_general(a, b, (dims, ((), ())), precision=HIGHEST, preferred_element_type=F32)
-
-    half = size // n_rep
-    own = back[pl.ds(pl.multiple_of(rep_ref[0] * half, half), half), :]
-    basis_ref[...] = factor * dot(own, block_ref[...].astype(F32), ((1,), (1,)))
-    ritz_ref[...] = factor * dot(dot(inverse, cross_ref[...], ((1,), (0,))), inverse, ((1,), (1,)))
 
 
 def solution(mesh):
@@ -291,13 +307,14 @@
             name="assemble",
         )(tile_rows, tile_cols, tile_scales, live_tiles, rep, tile_values)
         piece = count // n_group
-        gram, cross, filtered = pl.pallas_call(
-            functools.partial(exchange, n_row, n_col, n_rep),
+        factor = math.sqrt(local_rows * n_row * n_col)
+        return pl.pallas_call(
+            functools.partial(exchange, n_row, n_col, n_rep, factor),
             out_shape=(
-                shape((count, count), F32), shape((count, count), F32), shape((block, count), BF16),
+                shape((half_vec, local_rows), F32), shape((count, count), F32),
             ),
             in_specs=[vmem] * 4,
-            out_specs=(vmem,) * 3,
+            out_specs=(vmem,) * 2,
             scratch_shapes=[
                 pltpu.VMEM((n_group, half_vec, block), BF16),
                 pltpu.VMEM((n_col, lines, block), F32),
@@ -311,6 +328,8 @@
                 pltpu.VMEM((n_group, piece, count), F32),
                 pltpu.VMEM((n_col, piece, count), F32),
                 pltpu.VMEM((n_group, piece, count), F32),
+                pltpu.VMEM((count, 2 * count), F32),
+                pltpu.VMEM((count, count), F32),
                 pltpu.SemaphoreType.DMA((DEGREE + 4, n_group - 1)),
                 pltpu.SemaphoreType.DMA((DEGREE + 4, n_group - 1)),
                 pltpu.SemaphoreType.DMA((DEGREE + 3, n_col - 1)),
@@ -319,15 +338,6 @@
             compiler_params=pltpu.CompilerParams(collective_id=0, has_side_effects=True),
             name="exchange",
         )(high, low, degree, vectors)
-        factor = math.sqrt(local_rows * n_row * n_col)
-        return pl.pallas_call(
-            functools.partial(finish, n_rep, factor),
-            out_shape=(shape((half_vec, local_rows), F32), shape((count, count), F32)),
-            in_specs=[smem] + [vmem] * 3,
-            out_specs=(vmem,) * 2,
-            scratch_shapes=[pltpu.VMEM((count, count), F32), pltpu.VMEM((count, count), F32)],
-            name="finish",
-        )(rep, gram, cross, filtered)
 
     return jax.shard_map(
         shards,

time: 73.1 us -> 59.6 us (0.82)
  Pallas kernels: 71.6 us -> 55.2 us
  local copies, waits for them, and re-layouts: 0 us -> 2.85 us
    pallas_call x2 -> x1, Pallas kernels: 67.7 us -> 51.3 us  [shards(): pl.pallas_call(functools.partial(exchange, n_row, n_col, n_rep, factor),...]
    unnamed x0 -> x2, local copies, waits for them, and re-layouts: none -> 2.85 us
where the time goes in v2:
time: 59.6 us; the launch traced here: 59.3 us
  Pallas kernels  55.2 us (93%)
  local copies, waits for them, and re-layouts  2.85 us (5%)
  between operations  1.3 us (2%)
    pallas_call x1, Pallas kernels, shards(): pl.pallas_call(functools.partial(exchange, n_row, n_col, n_rep, factor),...  51.3 us
    pallas_call x1, Pallas kernels, shards(): pl.pallas_call(functools.partial(assemble, n_col, n_row, chunks), out_sha...  3.89 us
    unnamed x2, local copies, waits for them, and re-layouts  2.85 us

profile of v2, /device:TPU:0, one launch (start us, length us, event | category | flops | bytes accessed | tf_op | source)
XLA Modules:
  0.0 59.3 jit_solution(2400498876039878709)
XLA Ops:
  1.3 3.9 %assemble.1 = (bf16[512,256]{1,0:T(8,128)(2,1)}, bf16[512,256]{1,0:T(8,128)(2,1)}, f32[8,128]{1,0:T(8,128)}) custom-call(s32[144]{0:T(256)} %rows_ref.1, s32[144]{0:T(256)} %cols_ref.1, f32[144]{0:T(256)} %scales_ref.1, s32[1]{0:T(128)S(6)} %copy.10.live_ref, s32[1]{0:T(128)} %bitcast.rep_ref, bf16[144,128,128]{2,1,0:T(8,128)(2,1)} %tiles_ref.1), custom_call_target="tpu_custom_call" | custom-call | tf_op jit(solution)/shard_map/assemble/pallas_call | solution.py:292
  5.2 51.3 %exchange.1 = (f32[64,128]{1,0:T(8,128)}, f32[128,128]{1,0:T(8,128)}) custom-call(bf16[512,256]{1,0:T(8,128)(2,1)} %get-tuple-element.5.high_ref, bf16[512,256]{1,0:T(8,128)(2,1)} %get-tuple-element.6.low_ref, f32[8,128]{1,0:T(8,128)} %get-tuple-element.7.degree_ref, bf16[64,128]{1,0:T(8,128)(2,1)} %vectors_ref.1), custom_call_target="tpu_custom_call" | custom-call | tf_op jit(solution)/shard_map/exchange/pallas_call | solution.py:311
  56.5 1.4 %copy.11 = f32[64,128]{1,0:T(8,128)} copy(f32[64,128]{1,0:T(8,128)} %get-tuple-element.10) | data formatting | bytes 65536
  57.8 1.5 %copy.12 = f32[128,128]{1,0:T(8,128)} copy(f32[128,128]{1,0:T(8,128)} %get-tuple-element.11) | data formatting | bytes 131072

commit v3 on v2

--- a/solution.py
+++ b/solution.py
@@ -109,9 +109,9 @@
 
 
 def exchange(
-    n_row, n_col, n_rep, factor,
+    n_row, n_col, n_rep,
     high_ref, low_ref, degree_ref, vectors_ref,
-    basis_ref, ritz_ref,
+    inverse_ref, cross_ref, block_ref,
     raw, degrees, panels, sends, lands, owners, inv, grams, cross_send, cross_one, cross_two, cross_all, work, inverse,
     g_send, g_recv, c_send, c_recv,
 ):
@@ -150,12 +150,15 @@
         started.extend(out)
         return out
 
-    def to_col(phase, source, target):
+    side = n_col // 2
+    upper = lax.div(col, side)
+    far = [(1 - upper) * (n_col - 1 - s) + upper * s for s in range(n_col - side)]
+    near = [upper * side + lax.rem(col + s, side) for s in range(1, side)]
+
+    def to_col(phase, source, target, others):
         out = []
-        upper = lax.div(2 * col, n_col)
-        for s in range(n_col - 1):
-            k = (1 - upper) * (n_col - 1 - s) + upper * (1 + s)
-            other = lax.rem(col + k, n_col)
+        for other in others:
+            k = lax.rem(other - col + n_col, n_col)
             copy = pltpu.make_async_remote_copy(
                 src_ref=source(other), dst_ref=target,
                 send_sem=c_send.at[phase, k - 1], recv_sem=c_recv.at[phase, k - 1],
@@ -171,7 +174,7 @@
             copy.wait_recv()
 
     gathering = to_group(0, lambda m: vectors_ref, raw.at[me])
-    degree_moves = to_col(0, lambda m: degree_ref, degrees.at[col])
+    degree_moves = to_col(0, lambda m: degree_ref, degrees.at[col], far + near)
     raw[me] = vectors_ref[...]
     degrees[col] = degree_ref[...]
     arrive(gathering)
@@ -190,8 +193,15 @@
     previous = panels[0, me].astype(F32)
     current = previous
     for n in range(DEGREE):
-        sends[n] = products(n).astype(BF16).reshape(n_col, half, count)
-        moving = to_col(1 + n, lambda m: sends.at[n, m], lands.at[n, col])
+        moving = []
+        panel = panels[n].reshape(n_group * half, count)
+        for base, others in (((1 - upper) * side, far), (upper * side, near)):
+            part = pl.ds(pl.multiple_of(base * half, half), side * half)
+            partial = contract(high_ref[part, :], panel, ((1,), (0,))) + contract(
+                low_ref[part, :], panel, ((1,), (0,))
+            )
+            sends[n, pl.ds(base, side)] = partial.astype(BF16).reshape(side, half, count)
+            moving += to_col(1 + n, lambda m: sends.at[n, m], lands.at[n, col], others)
         if n == 0:
             arrive(degree_moves)
             sums = degrees[0]
@@ -218,7 +228,7 @@
         panels[n + 1, me] = rounded
         if n == DEGREE - 1:
             owners[col] = rounded
-            sharing = to_col(DEGREE + 1, lambda m: owners.at[col], owners.at[col])
+            sharing = to_col(DEGREE + 1, lambda m: owners.at[col], owners.at[col], far + near)
         gathering = to_group(1 + n, lambda m: panels.at[n + 1, me], panels.at[n + 1, me])
         arrive(gathering)
 
@@ -251,7 +261,7 @@
     for s in range(1, n_group):
         value = value + cross_one[s]
     cross_two[col] = value
-    moving = to_col(DEGREE + 2, lambda m: cross_two.at[col], cross_two.at[col])
+    moving = to_col(DEGREE + 2, lambda m: cross_two.at[col], cross_two.at[col], far + near)
     for band in range(1, bands - 2):
         eliminate(work, inverse, band)
     arrive(moving)
@@ -262,15 +272,22 @@
     moving = to_group(DEGREE + 3, lambda m: cross_all.at[me], cross_all.at[me])
     for band in range(bands - 2, bands):
         eliminate(work, inverse, band)
-    block = panels[DEGREE, pl.ds(row * n_rep, n_rep)].reshape(count, count).astype(F32)
-    own = inverse[pl.ds(pl.multiple_of(rep * half, half), half), :]
-    basis_ref[...] = factor * exact(own, block, ((1,), (1,)))
-    whole = inverse[...]
+    block_ref[...] = panels[DEGREE, pl.ds(row * n_rep, n_rep)].reshape(count, count)
+    inverse_ref[...] = inverse[...]
     arrive(moving)
-    left = exact(whole, cross_all[...].reshape(count, count), ((1,), (0,)))
-    ritz_ref[...] = factor * exact(left, whole, ((1,), (1,)))
+    cross_ref[...] = cross_all[...].reshape(count, count)
     for copy in started:
         copy.wait_send()
+
+
+def finish(n_rep, factor, rep_ref, inverse_ref, cross_ref, block_ref, basis_ref, ritz_ref):
+    size = inverse_ref.shape[0]
+    half = size // n_rep
+    whole = inverse_ref[...]
+    left = exact(whole, cross_ref[...], ((1,), (0,)))
+    own = inverse_ref[pl.ds(pl.multiple_of(rep_ref[0] * half, half), half), :]
+    basis_ref[...] = factor * exact(own, block_ref[...].astype(F32), ((1,), (1,)))
+    ritz_ref[...] = factor * exact(left, whole, ((1,), (1,)))
 
 
 def solution(mesh):
@@ -308,13 +325,13 @@
         )(tile_rows, tile_cols, tile_scales, live_tiles, rep, tile_values)
         piece = count // n_group
         factor = math.sqrt(local_rows * n_row * n_col)
-        return pl.pallas_call(
-            functools.partial(exchange, n_row, n_col, n_rep, factor),
+        inverse, cross, filtered = pl.pallas_call(
+            functools.partial(exchange, n_row, n_col, n_rep),
             out_shape=(
-                shape((half_vec, local_rows), F32), shape((count, count), F32),
+                shape((count, count), F32), shape((count, count), F32), shape((block, count), BF16),
             ),
             in_specs=[vmem] * 4,
-            out_specs=(vmem,) * 2,
+            out_specs=(vmem,) * 3,
             scratch_shapes=[
                 pltpu.VMEM((n_group, half_vec, block), BF16),
                 pltpu.VMEM((n_col, lines, block), F32),
@@ -338,6 +355,13 @@
             compiler_params=pltpu.CompilerParams(collective_id=0, has_side_effects=True),
             name="exchange",
         )(high, low, degree, vectors)
+        return pl.pallas_call(
+            functools.partial(finish, n_rep, factor),
+            out_shape=(shape((half_vec, local_rows), F32), shape((count, count), F32)),
+            in_specs=[smem] + [vmem] * 3,
+            out_specs=(vmem,) * 2,
+            name="finish",
+        )(rep, inverse, cross, filtered)
 
     return jax.shard_map(
         shards,

time: 59.6 us -> 60.4 us (1.013)
  Pallas kernels: 55.2 us -> 58.8 us
  local copies, waits for them, and re-layouts: 2.85 us -> 0 us
    pallas_call x1 -> x2, Pallas kernels: 51.3 us -> 55 us  [the longest x1 53 us: shards(): pl.pallas_call(functools.partial(exchange, n_row, n_col, n_rep), out_shap...]
    unnamed x2 -> x0, local copies, waits for them, and re-layouts: 2.85 us -> none
where the time goes in v3:
time: 60.4 us; the launch traced here: 60.1 us
  Pallas kernels  58.8 us (97%)
  between operations  1.3 us (2%)
    pallas_call x1, Pallas kernels, shards(): pl.pallas_call(functools.partial(exchange, n_row, n_col, n_rep), out_shap...  53 us
    pallas_call x1, Pallas kernels, shards(): pl.pallas_call(functools.partial(assemble, n_col, n_row, chunks), out_sha...  3.89 us
    pallas_call x1, Pallas kernels, shards(): pl.pallas_call(functools.partial(finish, n_rep, factor), out_shape=(shape...  1.99 us

profile of v3, /device:TPU:0, one launch (start us, length us, event | category | flops | bytes accessed | tf_op | source)
XLA Modules:
  0.0 60.1 jit_solution(5013722386284328602)
XLA Ops:
  1.3 3.9 %assemble.1 = (bf16[512,256]{1,0:T(8,128)(2,1)}, bf16[512,256]{1,0:T(8,128)(2,1)}, f32[8,128]{1,0:T(8,128)}) custom-call(s32[144]{0:T(256)} %rows_ref.1, s32[144]{0:T(256)} %cols_ref.1, f32[144]{0:T(256)} %scales_ref.1, s32[1]{0:T(128)S(6)} %copy.8.live_ref, s32[1]{0:T(128)} %bitcast.rep_ref, bf16[144,128,128]{2,1,0:T(8,128)(2,1)} %tiles_ref.1), custom_call_target="tpu_custom_call" | custom-call | tf_op jit(solution)/shard_map/assemble/pallas_call | solution.py:309
  5.2 53.0 %exchange.1 = (f32[128,128]{1,0:T(8,128)}, f32[128,128]{1,0:T(8,128)}, bf16[128,128]{1,0:T(8,128)(2,1)}) custom-call(bf16[512,256]{1,0:T(8,128)(2,1)} %get-tuple-element.8.high_ref, bf16[512,256]{1,0:T(8,128)(2,1)} %get-tuple-element.9.low_ref, f32[8,128]{1,0:T(8,128)} %get-tuple-element.10.degree_ref, bf16[64,128]{1,0:T(8,128)(2,1)} %vectors_ref.1), custom_call_target="tpu_custom_call" | custom-call | tf_op jit(solution)/shard_map/exchange/pallas_call | solution.py:328
  58.2 2.0 %finish.1 = (f32[64,128]{1,0:T(8,128)}, f32[128,128]{1,0:T(8,128)}) custom-call(s32[1]{0:T(128)} %bitcast.rep_ref, f32[128,128]{1,0:T(8,128)} %get-tuple-element.11.inverse_ref, f32[128,128]{1,0:T(8,128)} %get-tuple-element.12.cross_ref, bf16[128,128]{1,0:T(8,128)(2,1)} %get-tuple-element.13.block_ref), custom_call_target="tpu_custom_call" | custom-call | tf_op jit(solution)/shard_map/finish/pallas_call | solution.py:358

commit v4 on v3

--- a/solution.py
+++ b/solution.py
@@ -150,15 +150,12 @@
         started.extend(out)
         return out
 
-    side = n_col // 2
-    upper = lax.div(col, side)
-    far = [(1 - upper) * (n_col - 1 - s) + upper * s for s in range(n_col - side)]
-    near = [upper * side + lax.rem(col + s, side) for s in range(1, side)]
-
-    def to_col(phase, source, target, others):
+    def to_col(phase, source, target):
         out = []
-        for other in others:
-            k = lax.rem(other - col + n_col, n_col)
+        upper = lax.div(2 * col, n_col)
+        for s in range(n_col - 1):
+            k = (1 - upper) * (n_col - 1 - s) + upper * (1 + s)
+            other = lax.rem(col + k, n_col)
             copy = pltpu.make_async_remote_copy(
                 src_ref=source(other), dst_ref=target,
                 send_sem=c_send.at[phase, k - 1], recv_sem=c_recv.at[phase, k - 1],
@@ -174,7 +171,7 @@
             copy.wait_recv()
 
     gathering = to_group(0, lambda m: vectors_ref, raw.at[me])
-    degree_moves = to_col(0, lambda m: degree_ref, degrees.at[col], far + near)
+    degree_moves = to_col(0, lambda m: degree_ref, degrees.at[col])
     raw[me] = vectors_ref[...]
     degrees[col] = degree_ref[...]
     arrive(gathering)
@@ -193,15 +190,8 @@
     previous = panels[0, me].astype(F32)
     current = previous
     for n in range(DEGREE):
-        moving = []
-        panel = panels[n].reshape(n_group * half, count)
-        for base, others in (((1 - upper) * side, far), (upper * side, near)):
-            part = pl.ds(pl.multiple_of(base * half, half), side * half)
-            partial = contract(high_ref[part, :], panel, ((1,), (0,))) + contract(
-                low_ref[part, :], panel, ((1,), (0,))
-            )
-            sends[n, pl.ds(base, side)] = partial.astype(BF16).reshape(side, half, count)
-            moving += to_col(1 + n, lambda m: sends.at[n, m], lands.at[n, col], others)
+        sends[n] = products(n).astype(BF16).reshape(n_col, half, count)
+        moving = to_col(1 + n, lambda m: sends.at[n, m], lands.at[n, col])
         if n == 0:
             arrive(degree_moves)
             sums = degrees[0]
@@ -228,7 +218,7 @@
         panels[n + 1, me] = rounded
         if n == DEGREE - 1:
             owners[col] = rounded
-            sharing = to_col(DEGREE + 1, lambda m: owners.at[col], owners.at[col], far + near)
+            sharing = to_col(DEGREE + 1, lambda m: owners.at[col], owners.at[col])
         gathering = to_group(1 + n, lambda m: panels.at[n + 1, me], panels.at[n + 1, me])
         arrive(gathering)
 
@@ -261,7 +251,7 @@
     for s in range(1, n_group):
         value = value + cross_one[s]
     cross_two[col] = value
-    moving = to_col(DEGREE + 2, lambda m: cross_two.at[col], cross_two.at[col], far + near)
+    moving = to_col(DEGREE + 2, lambda m: cross_two.at[col], cross_two.at[col])
     for band in range(1, bands - 2):
         eliminate(work, inverse, band)
     arrive(moving)

time: 60.4 us -> 61 us (level)
  Pallas kernels: 58.8 us -> 59.5 us
    pallas_call x1, Pallas kernels: 53 us -> 53.6 us  [shards(): pl.pallas_call(functools.partial(exchange, n_row, n_col, n_rep), out_shap...]
where the time goes in v4:
time: 61 us; the launch traced here: 60.8 us
  Pallas kernels  59.5 us (98%)
  between operations  1.3 us (2%)
    pallas_call x1, Pallas kernels, shards(): pl.pallas_call(functools.partial(exchange, n_row, n_col, n_rep), out_shap...  53.6 us
    pallas_call x1, Pallas kernels, shards(): pl.pallas_call(functools.partial(assemble, n_col, n_row, chunks), out_sha...  3.89 us
    pallas_call x1, Pallas kernels, shards(): pl.pallas_call(functools.partial(finish, n_rep, factor), out_shape=(shape...  1.99 us

profile of v4, /device:TPU:0, one launch (start us, length us, event | category | flops | bytes accessed | tf_op | source)
XLA Modules:
  0.0 60.8 jit_solution(13309139688722806431)
XLA Ops:
  1.3 3.9 %assemble.1 = (bf16[512,256]{1,0:T(8,128)(2,1)}, bf16[512,256]{1,0:T(8,128)(2,1)}, f32[8,128]{1,0:T(8,128)}) custom-call(s32[144]{0:T(256)} %rows_ref.1, s32[144]{0:T(256)} %cols_ref.1, f32[144]{0:T(256)} %scales_ref.1, s32[1]{0:T(128)S(6)} %copy.8.live_ref, s32[1]{0:T(128)} %bitcast.rep_ref, bf16[144,128,128]{2,1,0:T(8,128)(2,1)} %tiles_ref.1), custom_call_target="tpu_custom_call" | custom-call | tf_op jit(solution)/shard_map/assemble/pallas_call | solution.py:299
  5.2 53.6 %exchange.1 = (f32[128,128]{1,0:T(8,128)}, f32[128,128]{1,0:T(8,128)}, bf16[128,128]{1,0:T(8,128)(2,1)}) custom-call(bf16[512,256]{1,0:T(8,128)(2,1)} %get-tuple-element.8.high_ref, bf16[512,256]{1,0:T(8,128)(2,1)} %get-tuple-element.9.low_ref, f32[8,128]{1,0:T(8,128)} %get-tuple-element.10.degree_ref, bf16[64,128]{1,0:T(8,128)(2,1)} %vectors_ref.1), custom_call_target="tpu_custom_call" | custom-call | tf_op jit(solution)/shard_map/exchange/pallas_call | solution.py:318
  58.8 2.0 %finish.1 = (f32[64,128]{1,0:T(8,128)}, f32[128,128]{1,0:T(8,128)}) custom-call(s32[1]{0:T(128)} %bitcast.rep_ref, f32[128,128]{1,0:T(8,128)} %get-tuple-element.11.inverse_ref, f32[128,128]{1,0:T(8,128)} %get-tuple-element.12.cross_ref, bf16[128,128]{1,0:T(8,128)(2,1)} %get-tuple-element.13.block_ref), custom_call_target="tpu_custom_call" | custom-call | tf_op jit(solution)/shard_map/finish/pallas_call | solution.py:348
